TPU v7x, 32 devices: a whole 2x2x4 slice. The times are simulated.
32 devices in a mesh: dp: 2 (over x), pipe: 4 (over z), mp: 4 (over y, core).
Axes of the slice: x: 2, y: 2, z: 4, core: 2. Of those that a mesh axis runs over, the one named last changes fastest.
Arguments:
- inputs: bfloat16 [4, 128, 1024], P(None, 'dp', 'mp'), may hold values from -6 to 6
- cotangent: bfloat16 [4, 128, 1024], P(None, 'dp', 'mp'), may hold values from -6 to 6
- gain: float32 [4, 1024], P('pipe'), may hold values from 0.25 to 1.75
- weight_in: bfloat16 [4, 1024, 32768], P('pipe', None, 'mp'), may hold values from -0.1875 to 0.1875
- weight_out: bfloat16 [4, 32768, 1024], P('pipe', 'mp'), may hold values from -0.03125 to 0.03125
Outputs:
- grad_in: bfloat16 [4, 1024, 32768], P('pipe', 'dp', 'mp')
- grad_out: bfloat16 [4, 32768, 1024], P('pipe', 'mp', 'dp')
- grad_gain: float32 [4, 1024], P('pipe', 'mp')
All inputs are finite; a program needn't handle non-finite values.
Results may differ from a plain program's by a relative error of at most 0.023.
Values may be sent and summed in bfloat16 or wider, within the bound.
A program may use at most 128 MiB of HBM per device.

v0:
```python
import math
import jax
import jax.numpy as jnp
from jax import lax
from jax.sharding import PartitionSpec as P

GELU_COEF = math.sqrt(2.0 / math.pi)
CUBIC_COEF = 0.044715
NORM_EPS = 1e-06
CONTRACT_LAST = (((1,), (1,)), ((), ()))
CONTRACT_FIRST = (((0,), (0,)), ((), ()))


def shifted(shard, axis, by):
    count = lax.axis_size(axis)
    pairs = [(i, i + by) for i in range(count) if 0 <= i + by < count]
    return lax.ppermute(shard, axis, pairs)


def gelu_parts(values):
    tangent = jnp.tanh(GELU_COEF * (values + CUBIC_COEF * values * values * values))
    output = 0.5 * values * (1.0 + tangent)
    derivative = 0.5 * (1.0 + tangent) + 0.5 * values * (1.0 - tangent * tangent) * GELU_COEF * (
        1.0 + 3.0 * CUBIC_COEF * values * values
    )
    return (output, derivative)


def shards(inputs, cotangent, gain, weight_in, weight_out):
    segment_count = lax.axis_size("pipe")
    section = lax.axis_index("pipe")
    part_index = lax.axis_index("mp")
    replicas = lax.axis_size("dp")
    micro, row_count, width = inputs.shape
    weight_first = weight_in[0]
    weight_second = weight_out[0]
    gain_row = gain[0]
    full_width = gain_row.shape[0]
    hidden = weight_first.shape[1]
    gain_own = lax.dynamic_slice_in_dim(gain_row, part_index * width, width, 0)
    turns = segment_count + micro - 1

    def forward_turn(turn, carry):
        incoming, rows_save, scale_save, gate_save = carry
        micro_slot = turn - section
        is_active = (micro_slot >= 0) & (micro_slot < micro)
        slot_index = jnp.clip(micro_slot, 0, micro - 1)
        first_rows = lax.dynamic_index_in_dim(inputs, slot_index, 0, keepdims=False)
        segment_input = jnp.where(section == 0, first_rows, incoming)
        whole_rows = lax.all_gather(segment_input, "mp", axis=1, tiled=True)

        def forward_active(operands):
            gathered, rows_keep, scale_keep, gate_keep = operands
            values = gathered.astype(jnp.float32)
            inv_rms = lax.rsqrt(jnp.mean(values * values, axis=1) + NORM_EPS)
            normed = (values * inv_rms[:, None] * gain_row).astype(jnp.bfloat16)
            gate_input = jnp.dot(normed, weight_first, preferred_element_type=jnp.float32)
            activated = gelu_parts(gate_input)[0].astype(jnp.bfloat16)
            branch = jnp.dot(activated, weight_second, preferred_element_type=jnp.float32)
            rows_keep = lax.dynamic_update_index_in_dim(rows_keep, gathered, slot_index, 0)
            scale_keep = lax.dynamic_update_index_in_dim(scale_keep, inv_rms, slot_index, 0)
            gate_keep = lax.dynamic_update_index_in_dim(gate_keep, gate_input, slot_index, 0)
            return (branch, rows_keep, scale_keep, gate_keep)

        def forward_resting(operands):
            gathered, rows_keep, scale_keep, gate_keep = operands
            return (
                jnp.zeros((row_count, full_width), jnp.float32),
                rows_keep,
                scale_keep,
                gate_keep,
            )

        branch, rows_save, scale_save, gate_save = lax.cond(
            is_active,
            forward_active,
            forward_resting,
            (whole_rows, rows_save, scale_save, gate_save),
        )
        branch_sum = lax.psum_scatter(branch, "mp", scatter_dimension=1, tiled=True)
        result = (segment_input.astype(jnp.float32) + branch_sum).astype(jnp.bfloat16)
        passed = shifted(result, "pipe", 1)
        return (passed, rows_save, scale_save, gate_save)

    forward_init = (
        jnp.zeros((row_count, width), jnp.bfloat16),
        jnp.zeros((micro, row_count, full_width), jnp.bfloat16),
        jnp.zeros((micro, row_count), jnp.float32),
        jnp.zeros((micro, row_count, hidden), jnp.float32),
    )
    forward_out = lax.fori_loop(0, turns, forward_turn, forward_init)
    rows_save = forward_out[1]
    scale_save = forward_out[2]
    gate_save = forward_out[3]

    def backward_turn(turn, carry):
        incoming, pregrad_save, outgrad_save, gain_acc = carry
        micro_slot = turn - (segment_count - 1 - section)
        is_active = (micro_slot >= 0) & (micro_slot < micro)
        slot_index = jnp.clip(micro_slot, 0, micro - 1)
        last_rows = lax.dynamic_index_in_dim(cotangent, slot_index, 0, keepdims=False).astype(
            jnp.float32
        )
        grad_rows = jnp.where(section == segment_count - 1, last_rows, incoming)
        whole_grad = lax.all_gather(grad_rows.astype(jnp.bfloat16), "mp", axis=1, tiled=True)

        def backward_active(operands):
            gathered, pregrad_keep, outgrad_keep = operands
            gate_input = lax.dynamic_index_in_dim(gate_save, slot_index, 0, keepdims=False)
            slopes = gelu_parts(gate_input)[1]
            inner_grad = lax.dot_general(
                gathered, weight_second, CONTRACT_LAST, preferred_element_type=jnp.float32
            )
            pre_grad = (inner_grad * slopes).astype(jnp.bfloat16)
            norm_part = lax.dot_general(
                pre_grad, weight_first, CONTRACT_LAST, preferred_element_type=jnp.float32
            )
            pregrad_keep = lax.dynamic_update_index_in_dim(pregrad_keep, pre_grad, slot_index, 0)
            outgrad_keep = lax.dynamic_update_index_in_dim(outgrad_keep, gathered, slot_index, 0)
            return (norm_part, pregrad_keep, outgrad_keep)

        def backward_resting(operands):
            gathered, pregrad_keep, outgrad_keep = operands
            return (jnp.zeros((row_count, full_width), jnp.float32), pregrad_keep, outgrad_keep)

        norm_part, pregrad_save, outgrad_save = lax.cond(
            is_active, backward_active, backward_resting, (whole_grad, pregrad_save, outgrad_save)
        )
        values = lax.dynamic_index_in_dim(rows_save, slot_index, 0, keepdims=False).astype(
            jnp.float32
        )
        inv_rms = lax.dynamic_index_in_dim(scale_save, slot_index, 0, keepdims=False)
        unit_full = values * inv_rms[:, None]
        unit_own = lax.dynamic_slice_in_dim(unit_full, part_index * width, width, 1)
        norm_grad = lax.psum_scatter(norm_part, "mp", scatter_dimension=1, tiled=True)
        scaled = norm_grad * gain_own
        row_dot = lax.psum(jnp.sum(scaled * unit_own, axis=1), "mp")
        previous = grad_rows + inv_rms[:, None] * (
            scaled - unit_own * row_dot[:, None] / full_width
        )
        gain_acc = gain_acc + jnp.where(is_active, jnp.sum(norm_grad * unit_own, axis=0), 0.0)
        passed = shifted(previous, "pipe", -1)
        return (passed, pregrad_save, outgrad_save, gain_acc)

    backward_init = (
        jnp.zeros((row_count, width), jnp.float32),
        jnp.zeros((micro, row_count, hidden), jnp.bfloat16),
        jnp.zeros((micro, row_count, full_width), jnp.bfloat16),
        jnp.zeros((width,), jnp.float32),
    )
    backward_out = lax.fori_loop(0, turns, backward_turn, backward_init)
    all_rows = micro * row_count
    pregrad_all = backward_out[1].reshape(all_rows, hidden)
    outgrad_all = backward_out[2].reshape(all_rows, full_width)
    gain_acc = backward_out[3]
    normed_all = (
        (rows_save.astype(jnp.float32) * scale_save[:, :, None] * gain_row)
        .astype(jnp.bfloat16)
        .reshape(all_rows, full_width)
    )
    activated_all = gelu_parts(gate_save)[0].astype(jnp.bfloat16).reshape(all_rows, hidden)
    half_width = full_width // replicas
    packed = jnp.stack((normed_all, outgrad_all)).reshape(2, all_rows, replicas, half_width)
    swapped = lax.all_to_all(packed, "dp", split_axis=2, concat_axis=1, tiled=True)
    columns = swapped.reshape(2, replicas * all_rows, half_width)
    pregrad_piece = lax.all_gather(pregrad_all, "dp", axis=0, tiled=True)
    activated_piece = lax.all_gather(activated_all, "dp", axis=0, tiled=True)
    normed_cols = columns[0]
    outgrad_cols = columns[1]
    in_term = lax.dot_general(
        normed_cols, pregrad_piece, CONTRACT_FIRST, preferred_element_type=jnp.float32
    )
    out_term = lax.dot_general(
        outgrad_cols, activated_piece, CONTRACT_FIRST, preferred_element_type=jnp.float32
    )
    grad_sums = jnp.stack((in_term, out_term))
    in_part = grad_sums[0]
    out_part = grad_sums[1]
    grad_first = in_part.astype(jnp.bfloat16)[None]
    grad_second = out_part.astype(jnp.bfloat16).T[None]
    gain_total = lax.psum(gain_acc, "dp")[None]
    return (grad_first, grad_second, gain_total)


def solution(mesh):
    in_specs = (
        P(None, "dp", "mp"),
        P(None, "dp", "mp"),
        P("pipe", None),
        P("pipe", None, "mp"),
        P("pipe", "mp", None),
    )
    out_specs = (P("pipe", "dp", "mp"), P("pipe", "mp", "dp"), P("pipe", "mp"))
    return jax.shard_map(shards, mesh=mesh, in_specs=in_specs, out_specs=out_specs, check_vma=False)
```

profile of v0, /device:TPU:0, one launch (start us, length us, event | category | flops | bytes accessed | tf_op | source)
XLA Modules:
  0.0 1032.1 jit_solution(17084897989914273569)
XLA Ops:
  13.2 334.4 %while.42 = (s32[]{:T(128)}, bf16[64,256]{1,0:T(8,128)(2,1)S(1)}, bf16[4,64,1024]{2,1,0:T(8,128)(2,1)S(1)}, f32[4,64]{1,0:T(4,128)S(1)}, f32[4,64,8192]{2,1,0:T(...) while((s32[]{:T(128)}, bf16[64,256]{1,0:T(8,128)(2,1)S(1)}, ...), condition=%wide.region_5.6_spmd, body=%wide.region_0.5_spmd.sunk | while | flops 2152726528 | bytes 110303480 | solution.py:91
  14.0 6.5 all_gather.28
  20.5 14.5 %conditional.5 = (f32[64,1024]{1,0:T(8,128)S(1)}, bf16[4,64,1024]{2,1,0:T(8,128)(2,1)S(1)}, f32[4,64]{1,0:T(4,128)S(1)}, f32[4,64,8192]{2,1,0:T(8,128)}) conditional(s32[]{:T(128)} %convert_element_type.141, (bf16[4,64,1024]{2,1,0:T(8,128)(2,1)S(1)}, f32[4,64]{1,0:T(4,128)S(1)}, f32[4,64,8192]{2,1,0:T(8,128)}) %tuple.97, ...), branch_computations={%region_1.1_spmd, %region_2.3_spmd} | conditional | flops 2152660992 | bytes 107747168 | solution.py:74
  20.7 10.4 %bitcast_dynamic-update-slice_fusion = (f32[4,64,8192]{2,1,0:T(8,128)}, f32[64,8192]{1,0:T(8,128)S(1)}) fusion(f32[4,64,8192]{2,1,0:T(8,128)} %get-tuple-element.578, s32[]{:T(128)S(6)} %select_n.85, bf16[1024,8192]{1,0:T(8,128)(2,1)} %get-tuple-element.573, bf16[64,1024]{1,0:T(8,128)(2,1)S(1)} %get-tuple-element.571, f32[1024]{0:T(1024)S(1)} %bitcast.78, ...), kind=kOutput, calls=%fused_computation.6 | convolution fusion | flops 1074003968 | bytes 21106948 | tf_op jit(solution)/shard_map/while/body/eval_jaxpr/cond/branch_1_fun/dot_general | solution.py:57
  35.8 18.8 %reduce-scatter.3.cloned.1.call-done = f32[64,256]{1,0:T(8,128)} async-done(((f32[64,1024]{1,0:T(8,128)}), f32[64,256]{1,0:T(8,128)}) %reduce-scatter.3.cloned.1.call-update) | async-done | bytes 65552 | tf_op jit(solution)/shard_map/while/body/eval_jaxpr/reduce_scatter | solution.py:80
  61.2 5.4 all_gather.28
  66.6 14.5 %conditional.5 = (f32[64,1024]{1,0:T(8,128)S(1)}, bf16[4,64,1024]{2,1,0:T(8,128)(2,1)S(1)}, f32[4,64]{1,0:T(4,128)S(1)}, f32[4,64,8192]{2,1,0:T(8,128)}) conditional(s32[]{:T(128)} %convert_element_type.141, (bf16[4,64,1024]{2,1,0:T(8,128)(2,1)S(1)}, f32[4,64]{1,0:T(4,128)S(1)}, f32[4,64,8192]{2,1,0:T(8,128)}) %tuple.97, ...), branch_computations={%region_1.1_spmd, %region_2.3_spmd} | conditional | flops 2152660992 | bytes 107747168 | solution.py:74
  66.7 10.4 %bitcast_dynamic-update-slice_fusion = (f32[4,64,8192]{2,1,0:T(8,128)}, f32[64,8192]{1,0:T(8,128)S(1)}) fusion(f32[4,64,8192]{2,1,0:T(8,128)} %get-tuple-element.578, s32[]{:T(128)S(6)} %select_n.85, bf16[1024,8192]{1,0:T(8,128)(2,1)} %get-tuple-element.573, bf16[64,1024]{1,0:T(8,128)(2,1)S(1)} %get-tuple-element.571, f32[1024]{0:T(1024)S(1)} %bitcast.78, ...), kind=kOutput, calls=%fused_computation.6 | convolution fusion | flops 1074003968 | bytes 21106948 | tf_op jit(solution)/shard_map/while/body/eval_jaxpr/cond/branch_1_fun/dot_general | solution.py:57
  81.9 19.2 %reduce-scatter.3.cloned.1.call-done = f32[64,256]{1,0:T(8,128)} async-done(((f32[64,1024]{1,0:T(8,128)}), f32[64,256]{1,0:T(8,128)}) %reduce-scatter.3.cloned.1.call-update) | async-done | bytes 65552 | tf_op jit(solution)/shard_map/while/body/eval_jaxpr/reduce_scatter | solution.py:80
  107.7 5.4 all_gather.28
  113.1 14.5 %conditional.5 = (f32[64,1024]{1,0:T(8,128)S(1)}, bf16[4,64,1024]{2,1,0:T(8,128)(2,1)S(1)}, f32[4,64]{1,0:T(4,128)S(1)}, f32[4,64,8192]{2,1,0:T(8,128)}) conditional(s32[]{:T(128)} %convert_element_type.141, (bf16[4,64,1024]{2,1,0:T(8,128)(2,1)S(1)}, f32[4,64]{1,0:T(4,128)S(1)}, f32[4,64,8192]{2,1,0:T(8,128)}) %tuple.97, ...), branch_computations={%region_1.1_spmd, %region_2.3_spmd} | conditional | flops 2152660992 | bytes 107747168 | solution.py:74
  113.2 10.4 %bitcast_dynamic-update-slice_fusion = (f32[4,64,8192]{2,1,0:T(8,128)}, f32[64,8192]{1,0:T(8,128)S(1)}) fusion(f32[4,64,8192]{2,1,0:T(8,128)} %get-tuple-element.578, s32[]{:T(128)S(6)} %select_n.85, bf16[1024,8192]{1,0:T(8,128)(2,1)} %get-tuple-element.573, bf16[64,1024]{1,0:T(8,128)(2,1)S(1)} %get-tuple-element.571, f32[1024]{0:T(1024)S(1)} %bitcast.78, ...), kind=kOutput, calls=%fused_computation.6 | convolution fusion | flops 1074003968 | bytes 21106948 | tf_op jit(solution)/shard_map/while/body/eval_jaxpr/cond/branch_1_fun/dot_general | solution.py:57
  128.4 20.1 %reduce-scatter.3.cloned.1.call-done = f32[64,256]{1,0:T(8,128)} async-done(((f32[64,1024]{1,0:T(8,128)}), f32[64,256]{1,0:T(8,128)}) %reduce-scatter.3.cloned.1.call-update) | async-done | bytes 65552 | tf_op jit(solution)/shard_map/while/body/eval_jaxpr/reduce_scatter | solution.py:80
  155.1 5.4 all_gather.28
  160.5 14.6 %conditional.5 = (f32[64,1024]{1,0:T(8,128)S(1)}, bf16[4,64,1024]{2,1,0:T(8,128)(2,1)S(1)}, f32[4,64]{1,0:T(4,128)S(1)}, f32[4,64,8192]{2,1,0:T(8,128)}) conditional(s32[]{:T(128)} %convert_element_type.141, (bf16[4,64,1024]{2,1,0:T(8,128)(2,1)S(1)}, f32[4,64]{1,0:T(4,128)S(1)}, f32[4,64,8192]{2,1,0:T(8,128)}) %tuple.97, ...), branch_computations={%region_1.1_spmd, %region_2.3_spmd} | conditional | flops 2152660992 | bytes 107747168 | solution.py:74
  160.6 10.3 %bitcast_dynamic-update-slice_fusion = (f32[4,64,8192]{2,1,0:T(8,128)}, f32[64,8192]{1,0:T(8,128)S(1)}) fusion(f32[4,64,8192]{2,1,0:T(8,128)} %get-tuple-element.578, s32[]{:T(128)S(6)} %select_n.85, bf16[1024,8192]{1,0:T(8,128)(2,1)} %get-tuple-element.573, bf16[64,1024]{1,0:T(8,128)(2,1)S(1)} %get-tuple-element.571, f32[1024]{0:T(1024)S(1)} %bitcast.78, ...), kind=kOutput, calls=%fused_computation.6 | convolution fusion | flops 1074003968 | bytes 21106948 | tf_op jit(solution)/shard_map/while/body/eval_jaxpr/cond/branch_1_fun/dot_general | solution.py:57
  175.8 21.0 %reduce-scatter.3.cloned.1.call-done = f32[64,256]{1,0:T(8,128)} async-done(((f32[64,1024]{1,0:T(8,128)}), f32[64,256]{1,0:T(8,128)}) %reduce-scatter.3.cloned.1.call-update) | async-done | bytes 65552 | tf_op jit(solution)/shard_map/while/body/eval_jaxpr/reduce_scatter | solution.py:80
  203.4 5.4 all_gather.28
  209.6 35.6 %reduce-scatter.3.cloned.1.call-done = f32[64,256]{1,0:T(8,128)} async-done(((f32[64,1024]{1,0:T(8,128)}), f32[64,256]{1,0:T(8,128)}) %reduce-scatter.3.cloned.1.call-update) | async-done | bytes 65552 | tf_op jit(solution)/shard_map/while/body/eval_jaxpr/reduce_scatter | solution.py:80
  251.7 5.4 all_gather.28
  257.9 35.6 %reduce-scatter.3.cloned.1.call-done = f32[64,256]{1,0:T(8,128)} async-done(((f32[64,1024]{1,0:T(8,128)}), f32[64,256]{1,0:T(8,128)}) %reduce-scatter.3.cloned.1.call-update) | async-done | bytes 65552 | tf_op jit(solution)/shard_map/while/body/eval_jaxpr/reduce_scatter | solution.py:80
  300.0 5.4 all_gather.28
  306.2 35.6 %reduce-scatter.3.cloned.1.call-done = f32[64,256]{1,0:T(8,128)} async-done(((f32[64,1024]{1,0:T(8,128)}), f32[64,256]{1,0:T(8,128)}) %reduce-scatter.3.cloned.1.call-update) | async-done | bytes 65552 | tf_op jit(solution)/shard_map/while/body/eval_jaxpr/reduce_scatter | solution.py:80
  347.6 6.1 fusion.48
  356.2 443.4 %while.43 = (s32[]{:T(128)}, f32[64,256]{1,0:T(8,128)S(1)}, bf16[4,64,8192]{2,1,0:T(8,128)(2,1)}, bf16[4,64,1024]{2,1,0:T(8,128)(2,1)S(1)}, f32[256]{0:T(256)S(1...) while((s32[]{:T(128)}, f32[64,256]{1,0:T(8,128)S(1)}, ...), condition=%wide.region_13.14_spmd.clone, body=%wide.region_6.13_spmd.clone.sunk | while | flops 2157756928 | bytes 42672648 | solution.py:151
  356.5 5.4 all_gather.29
  362.7 44.6 %reduce-scatter.5.cloned.1.call-done = f32[64,256]{1,0:T(8,128)} async-done(((f32[64,1024]{1,0:T(8,128)}), f32[64,256]{1,0:T(8,128)}) %reduce-scatter.5.cloned.1.call-update) | async-done | bytes 65552 | tf_op jit(solution)/shard_map/while/body/eval_jaxpr/reduce_scatter | solution.py:135
  408.4 5.8 psum.23
  416.4 4.8 collective-permute-done.1
  421.2 5.4 all_gather.29
  427.5 43.4 %reduce-scatter.5.cloned.1.call-done = f32[64,256]{1,0:T(8,128)} async-done(((f32[64,1024]{1,0:T(8,128)}), f32[64,256]{1,0:T(8,128)}) %reduce-scatter.5.cloned.1.call-update) | async-done | bytes 65552 | tf_op jit(solution)/shard_map/while/body/eval_jaxpr/reduce_scatter | solution.py:135
  471.9 5.8 psum.23
  484.8 5.4 all_gather.29
  491.0 43.4 %reduce-scatter.5.cloned.1.call-done = f32[64,256]{1,0:T(8,128)} async-done(((f32[64,1024]{1,0:T(8,128)}), f32[64,256]{1,0:T(8,128)}) %reduce-scatter.5.cloned.1.call-update) | async-done | bytes 65552 | tf_op jit(solution)/shard_map/while/body/eval_jaxpr/reduce_scatter | solution.py:135
  535.4 5.8 psum.23
  548.3 5.4 all_gather.29
  553.7 23.6 %conditional.6 = (f32[64,1024]{1,0:T(8,128)S(1)}, bf16[4,64,8192]{2,1,0:T(8,128)(2,1)}, bf16[4,64,1024]{2,1,0:T(8,128)(2,1)S(1)}) conditional(s32[]{:T(128)} %convert_element_type.142, (bf16[4,64,8192]{2,1,0:T(8,128)(2,1)}, bf16[4,64,1024]{2,1,0:T(8,128)(2,1)S(1)}) %tuple.101, (bf16[64,1024]{1,0:T(8,128)(2,1)S(1)}, bf16[8192,1024]{1,0:T(8,128)(2,1)}, ...), branch_computations={%region_7.7_spmd, %region_8.8_spmd} | conditional | flops 2157445120 | bytes 39452740 | solution.py:126
  553.7 12.6 %bitcast_dynamic-update-slice_fusion.2 = (bf16[4,64,8192]{2,1,0:T(8,128)(2,1)}, bf16[64,8192]{1,0:T(8,128)(2,1)S(1)}) fusion(bf16[4,64,8192]{2,1,0:T(8,128)(2,1)} %get-tuple-element.602, s32[]{:T(128)S(6)} %select_n.88, f32[4,64,8192]{2,1,0:T(8,128)} %get-tuple-element.599, bf16[64,1024]{1,0:T(8,128)(2,1)S(1)} %get-tuple-element.597, ...), kind=kOutput, calls=%fused_computation.41 | convolution fusion | flops 1083703296 | bytes 21102596 | tf_op jit(solution)/shard_map/while/body/eval_jaxpr/cond/branch_1_fun/dot_general | solution.py:111
  566.4 11.0 %fusion.50 = f32[64,1024]{1,0:T(8,128)S(1)} fusion(bf16[64,8192]{1,0:T(8,128)(2,1)S(1)} %get-tuple-element.748, bf16[1024,8192]{1,0:T(8,128)(2,1)} %get-tuple-element.601), kind=kOutput, calls=%fused_computation.74 | convolution fusion | flops 1073741824 | bytes 18087936 | tf_op jit(solution)/shard_map/while/body/eval_jaxpr/cond/branch_1_fun/dot_general | solution.py:115
  578.1 19.8 %reduce-scatter.5.cloned.1.call-done = f32[64,256]{1,0:T(8,128)} async-done(((f32[64,1024]{1,0:T(8,128)}), f32[64,256]{1,0:T(8,128)}) %reduce-scatter.5.cloned.1.call-update) | async-done | bytes 65552 | tf_op jit(solution)/shard_map/while/body/eval_jaxpr/reduce_scatter | solution.py:135
  598.9 5.8 psum.23
  611.8 5.4 all_gather.29
  617.2 23.6 %conditional.6 = (f32[64,1024]{1,0:T(8,128)S(1)}, bf16[4,64,8192]{2,1,0:T(8,128)(2,1)}, bf16[4,64,1024]{2,1,0:T(8,128)(2,1)S(1)}) conditional(s32[]{:T(128)} %convert_element_type.142, (bf16[4,64,8192]{2,1,0:T(8,128)(2,1)}, bf16[4,64,1024]{2,1,0:T(8,128)(2,1)S(1)}) %tuple.101, (bf16[64,1024]{1,0:T(8,128)(2,1)S(1)}, bf16[8192,1024]{1,0:T(8,128)(2,1)}, ...), branch_computations={%region_7.7_spmd, %region_8.8_spmd} | conditional | flops 2157445120 | bytes 39452740 | solution.py:126
  617.2 12.6 %bitcast_dynamic-update-slice_fusion.2 = (bf16[4,64,8192]{2,1,0:T(8,128)(2,1)}, bf16[64,8192]{1,0:T(8,128)(2,1)S(1)}) fusion(bf16[4,64,8192]{2,1,0:T(8,128)(2,1)} %get-tuple-element.602, s32[]{:T(128)S(6)} %select_n.88, f32[4,64,8192]{2,1,0:T(8,128)} %get-tuple-element.599, bf16[64,1024]{1,0:T(8,128)(2,1)S(1)} %get-tuple-element.597, ...), kind=kOutput, calls=%fused_computation.41 | convolution fusion | flops 1083703296 | bytes 21102596 | tf_op jit(solution)/shard_map/while/body/eval_jaxpr/cond/branch_1_fun/dot_general | solution.py:111
  629.9 10.9 %fusion.50 = f32[64,1024]{1,0:T(8,128)S(1)} fusion(bf16[64,8192]{1,0:T(8,128)(2,1)S(1)} %get-tuple-element.748, bf16[1024,8192]{1,0:T(8,128)(2,1)} %get-tuple-element.601), kind=kOutput, calls=%fused_computation.74 | convolution fusion | flops 1073741824 | bytes 18087936 | tf_op jit(solution)/shard_map/while/body/eval_jaxpr/cond/branch_1_fun/dot_general | solution.py:115
  641.6 19.8 %reduce-scatter.5.cloned.1.call-done = f32[64,256]{1,0:T(8,128)} async-done(((f32[64,1024]{1,0:T(8,128)}), f32[64,256]{1,0:T(8,128)}) %reduce-scatter.5.cloned.1.call-update) | async-done | bytes 65552 | tf_op jit(solution)/shard_map/while/body/eval_jaxpr/reduce_scatter | solution.py:135
  662.5 5.8 psum.23
  675.4 5.4 all_gather.29
  680.8 23.6 %conditional.6 = (f32[64,1024]{1,0:T(8,128)S(1)}, bf16[4,64,8192]{2,1,0:T(8,128)(2,1)}, bf16[4,64,1024]{2,1,0:T(8,128)(2,1)S(1)}) conditional(s32[]{:T(128)} %convert_element_type.142, (bf16[4,64,8192]{2,1,0:T(8,128)(2,1)}, bf16[4,64,1024]{2,1,0:T(8,128)(2,1)S(1)}) %tuple.101, (bf16[64,1024]{1,0:T(8,128)(2,1)S(1)}, bf16[8192,1024]{1,0:T(8,128)(2,1)}, ...), branch_computations={%region_7.7_spmd, %region_8.8_spmd} | conditional | flops 2157445120 | bytes 39452740 | solution.py:126
  680.8 12.6 %bitcast_dynamic-update-slice_fusion.2 = (bf16[4,64,8192]{2,1,0:T(8,128)(2,1)}, bf16[64,8192]{1,0:T(8,128)(2,1)S(1)}) fusion(bf16[4,64,8192]{2,1,0:T(8,128)(2,1)} %get-tuple-element.602, s32[]{:T(128)S(6)} %select_n.88, f32[4,64,8192]{2,1,0:T(8,128)} %get-tuple-element.599, bf16[64,1024]{1,0:T(8,128)(2,1)S(1)} %get-tuple-element.597, ...), kind=kOutput, calls=%fused_computation.41 | convolution fusion | flops 1083703296 | bytes 21102596 | tf_op jit(solution)/shard_map/while/body/eval_jaxpr/cond/branch_1_fun/dot_general | solution.py:111
  693.4 11.0 %fusion.50 = f32[64,1024]{1,0:T(8,128)S(1)} fusion(bf16[64,8192]{1,0:T(8,128)(2,1)S(1)} %get-tuple-element.748, bf16[1024,8192]{1,0:T(8,128)(2,1)} %get-tuple-element.601), kind=kOutput, calls=%fused_computation.74 | convolution fusion | flops 1073741824 | bytes 18087936 | tf_op jit(solution)/shard_map/while/body/eval_jaxpr/cond/branch_1_fun/dot_general | solution.py:115
  705.2 18.9 %reduce-scatter.5.cloned.1.call-done = f32[64,256]{1,0:T(8,128)} async-done(((f32[64,1024]{1,0:T(8,128)}), f32[64,256]{1,0:T(8,128)}) %reduce-scatter.5.cloned.1.call-update) | async-done | bytes 65552 | tf_op jit(solution)/shard_map/while/body/eval_jaxpr/reduce_scatter | solution.py:135
  725.1 5.8 psum.23
  738.0 5.4 all_gather.29
  743.4 23.6 %conditional.6 = (f32[64,1024]{1,0:T(8,128)S(1)}, bf16[4,64,8192]{2,1,0:T(8,128)(2,1)}, bf16[4,64,1024]{2,1,0:T(8,128)(2,1)S(1)}) conditional(s32[]{:T(128)} %convert_element_type.142, (bf16[4,64,8192]{2,1,0:T(8,128)(2,1)}, bf16[4,64,1024]{2,1,0:T(8,128)(2,1)S(1)}) %tuple.101, (bf16[64,1024]{1,0:T(8,128)(2,1)S(1)}, bf16[8192,1024]{1,0:T(8,128)(2,1)}, ...), branch_computations={%region_7.7_spmd, %region_8.8_spmd} | conditional | flops 2157445120 | bytes 39452740 | solution.py:126
  743.4 12.6 %bitcast_dynamic-update-slice_fusion.2 = (bf16[4,64,8192]{2,1,0:T(8,128)(2,1)}, bf16[64,8192]{1,0:T(8,128)(2,1)S(1)}) fusion(bf16[4,64,8192]{2,1,0:T(8,128)(2,1)} %get-tuple-element.602, s32[]{:T(128)S(6)} %select_n.88, f32[4,64,8192]{2,1,0:T(8,128)} %get-tuple-element.599, bf16[64,1024]{1,0:T(8,128)(2,1)S(1)} %get-tuple-element.597, ...), kind=kOutput, calls=%fused_computation.41 | convolution fusion | flops 1083703296 | bytes 21102596 | tf_op jit(solution)/shard_map/while/body/eval_jaxpr/cond/branch_1_fun/dot_general | solution.py:111
  756.0 11.0 %fusion.50 = f32[64,1024]{1,0:T(8,128)S(1)} fusion(bf16[64,8192]{1,0:T(8,128)(2,1)S(1)} %get-tuple-element.748, bf16[1024,8192]{1,0:T(8,128)(2,1)} %get-tuple-element.601), kind=kOutput, calls=%fused_computation.74 | convolution fusion | flops 1073741824 | bytes 18087936 | tf_op jit(solution)/shard_map/while/body/eval_jaxpr/cond/branch_1_fun/dot_general | solution.py:115
  767.8 18.0 %reduce-scatter.5.cloned.1.call-done = f32[64,256]{1,0:T(8,128)} async-done(((f32[64,1024]{1,0:T(8,128)}), f32[64,256]{1,0:T(8,128)}) %reduce-scatter.5.cloned.1.call-update) | async-done | bytes 65552 | tf_op jit(solution)/shard_map/while/body/eval_jaxpr/reduce_scatter | solution.py:135
  786.8 5.8 psum.23
  808.0 21.2 %psum.20 = f32[1,256]{1,0:T(1,128)} all-reduce(f32[1,256]{1,0:T(1,128)S(1)} %bitcast.82), channel_id=1, replica_groups=mesh['dp'=2,'pipe'=4,'mp'=4] {'dp'}, use_global_device_ids=true, to_apply=%region_14.15 | all-reduce | flops 256 | bytes 2048 | tf_op jit(solution)/shard_map/psum | solution.py:181
  829.4 81.4 %all-gather.5.cloned.1.call-done = bf16[512,8192]{1,0:T(8,128)(2,1)} async-done(((bf16[256,8192]{1,0:T(8,128)(2,1)}), bf16[512,8192]{1,0:T(8,128)(2,1)}) %all-gather.5.cloned.1.call-update) | async-done | bytes 8388624 | tf_op jit(solution)/shard_map/all_gather | solution.py:167
  910.8 10.5 %fusion.43 = bf16[1,8192,512]{2,1,0:T(8,128)(2,1)} fusion(bf16[512,8192]{1,0:T(8,128)(2,1)} %all-gather.5.cloned.1.call-done, bf16[512,512]{1,0:T(8,128)(2,1)S(1)} %bitcast.80), kind=kOutput, calls=%fused_computation.63 | convolution fusion | flops 4299161600 | bytes 17301504 | tf_op jit(solution)/shard_map/dot_general | solution.py:173
  921.3 93.5 %all-gather.3.cloned.1.call-done = bf16[512,8192]{1,0:T(8,128)(2,1)} async-done(((bf16[256,8192]{1,0:T(8,128)(2,1)}), bf16[512,8192]{1,0:T(8,128)(2,1)}) %all-gather.3.cloned.1.call-update) | async-done | bytes 8388624 | tf_op jit(solution)/shard_map/all_gather | solution.py:166
  1014.8 10.2 fusion.42
  (209 shorter events, 141.4 us)
Async XLA Ops:
  8.7 4.5 copy-start.3
  13.2 41.4 %reduce-scatter.3.cloned.1.call-start = ((), (), s32[]{:S(2)}) async-start(), calls=%async_computation.5 | async-start | bytes 327680 | tf_op jit(solution)/shard_map/while/body/eval_jaxpr/reduce_scatter | solution.py:80
  20.7 11.3 %copy-start = (bf16[8192,1024]{1,0:T(8,128)(2,1)S(1)}, bf16[8192,1024]{1,0:T(8,128)(2,1)}, u32[]{:S(2)}) copy-start(bf16[8192,1024]{1,0:T(8,128)(2,1)} %get-tuple-element.574) | copy-start | bytes 50331652 | tf_op jit(solution)/shard_map/while/body/eval_jaxpr/cond
  35.1 0.7 copy-start.1
  55.5 5.0 collective-permute-start
  60.4 40.7 %reduce-scatter.3.cloned.1.call-start = ((), (), s32[]{:S(2)}) async-start(), calls=%async_computation.5 | async-start | bytes 327680 | tf_op jit(solution)/shard_map/while/body/eval_jaxpr/reduce_scatter | solution.py:80
  66.7 11.3 %copy-start = (bf16[8192,1024]{1,0:T(8,128)(2,1)S(1)}, bf16[8192,1024]{1,0:T(8,128)(2,1)}, u32[]{:S(2)}) copy-start(bf16[8192,1024]{1,0:T(8,128)(2,1)} %get-tuple-element.574) | copy-start | bytes 50331652 | tf_op jit(solution)/shard_map/while/body/eval_jaxpr/cond
  81.1 0.7 copy-start.1
  102.0 5.0 collective-permute-start
  106.9 41.6 %reduce-scatter.3.cloned.1.call-start = ((), (), s32[]{:S(2)}) async-start(), calls=%async_computation.5 | async-start | bytes 327680 | tf_op jit(solution)/shard_map/while/body/eval_jaxpr/reduce_scatter | solution.py:80
  113.2 11.3 %copy-start = (bf16[8192,1024]{1,0:T(8,128)(2,1)S(1)}, bf16[8192,1024]{1,0:T(8,128)(2,1)}, u32[]{:S(2)}) copy-start(bf16[8192,1024]{1,0:T(8,128)(2,1)} %get-tuple-element.574) | copy-start | bytes 50331652 | tf_op jit(solution)/shard_map/while/body/eval_jaxpr/cond
  127.6 0.7 copy-start.1
  149.3 5.0 collective-permute-start
  154.3 42.5 %reduce-scatter.3.cloned.1.call-start = ((), (), s32[]{:S(2)}) async-start(), calls=%async_computation.5 | async-start | bytes 327680 | tf_op jit(solution)/shard_map/while/body/eval_jaxpr/reduce_scatter | solution.py:80
  160.6 11.3 %copy-start = (bf16[8192,1024]{1,0:T(8,128)(2,1)S(1)}, bf16[8192,1024]{1,0:T(8,128)(2,1)}, u32[]{:S(2)}) copy-start(bf16[8192,1024]{1,0:T(8,128)(2,1)} %get-tuple-element.574) | copy-start | bytes 50331652 | tf_op jit(solution)/shard_map/while/body/eval_jaxpr/cond
  175.0 0.7 copy-start.1
  197.7 5.0 collective-permute-start
  202.6 42.5 %reduce-scatter.3.cloned.1.call-start = ((), (), s32[]{:S(2)}) async-start(), calls=%async_computation.5 | async-start | bytes 327680 | tf_op jit(solution)/shard_map/while/body/eval_jaxpr/reduce_scatter | solution.py:80
  208.9 0.7 copy-start.1
  246.0 5.0 collective-permute-start
  251.0 42.5 %reduce-scatter.3.cloned.1.call-start = ((), (), s32[]{:S(2)}) async-start(), calls=%async_computation.5 | async-start | bytes 327680 | tf_op jit(solution)/shard_map/while/body/eval_jaxpr/reduce_scatter | solution.py:80
  257.2 0.7 copy-start.1
  294.3 5.0 collective-permute-start
  299.3 42.5 %reduce-scatter.3.cloned.1.call-start = ((), (), s32[]{:S(2)}) async-start(), calls=%async_computation.5 | async-start | bytes 327680 | tf_op jit(solution)/shard_map/while/body/eval_jaxpr/reduce_scatter | solution.py:80
  305.5 0.7 copy-start.1
  342.6 5.0 collective-permute-start
  353.7 2.6 copy-start.4
  356.4 50.9 %reduce-scatter.5.cloned.1.call-start = ((), (), s32[]{:S(2)}) async-start(), calls=%async_computation.6 | async-start | bytes 327680 | tf_op jit(solution)/shard_map/while/body/eval_jaxpr/reduce_scatter | solution.py:135
  362.0 0.7 copy-start.2
  415.1 6.2 collective-permute-start.1
  421.2 49.7 %reduce-scatter.5.cloned.1.call-start = ((), (), s32[]{:S(2)}) async-start(), calls=%async_computation.6 | async-start | bytes 327680 | tf_op jit(solution)/shard_map/while/body/eval_jaxpr/reduce_scatter | solution.py:135
  426.7 0.7 copy-start.2
  478.6 6.2 collective-permute-start.1
  484.8 49.6 %reduce-scatter.5.cloned.1.call-start = ((), (), s32[]{:S(2)}) async-start(), calls=%async_computation.6 | async-start | bytes 327680 | tf_op jit(solution)/shard_map/while/body/eval_jaxpr/reduce_scatter | solution.py:135
  490.2 0.7 copy-start.2
  542.1 6.2 collective-permute-start.1
  548.3 49.6 %reduce-scatter.5.cloned.1.call-start = ((), (), s32[]{:S(2)}) async-start(), calls=%async_computation.6 | async-start | bytes 327680 | tf_op jit(solution)/shard_map/while/body/eval_jaxpr/reduce_scatter | solution.py:135
  577.3 0.7 copy-start.2
  605.6 6.2 collective-permute-start.1
  611.8 49.7 %reduce-scatter.5.cloned.1.call-start = ((), (), s32[]{:S(2)}) async-start(), calls=%async_computation.6 | async-start | bytes 327680 | tf_op jit(solution)/shard_map/while/body/eval_jaxpr/reduce_scatter | solution.py:135
  640.9 0.7 copy-start.2
  669.2 6.2 collective-permute-start.1
  675.4 48.7 %reduce-scatter.5.cloned.1.call-start = ((), (), s32[]{:S(2)}) async-start(), calls=%async_computation.6 | async-start | bytes 327680 | tf_op jit(solution)/shard_map/while/body/eval_jaxpr/reduce_scatter | solution.py:135
  704.4 0.7 copy-start.2
  731.8 6.2 collective-permute-start.1
  738.0 47.8 %reduce-scatter.5.cloned.1.call-start = ((), (), s32[]{:S(2)}) async-start(), calls=%async_computation.6 | async-start | bytes 327680 | tf_op jit(solution)/shard_map/while/body/eval_jaxpr/reduce_scatter | solution.py:135
  767.0 0.7 copy-start.2
  793.5 6.2 collective-permute-start.1
  799.6 111.1 %all-gather.5.cloned.1.call-start = ((), (), s32[]{:S(2)}) async-start(), calls=%async_computation.4 | async-start | bytes 12582912 | tf_op jit(solution)/shard_map/all_gather | solution.py:167
  800.2 214.6 %all-gather.3.cloned.1.call-start = ((), (), s32[]{:S(2)}) async-start(), calls=%async_computation.3 | async-start | bytes 12582912 | tf_op jit(solution)/shard_map/all_gather | solution.py:166
  804.4 24.9 %all-to-all-start = ((bf16[2,256,2,512]{3,1,0,2:T(8,128)(2,1)}), bf16[2,256,2,512]{3,1,0,2:T(8,128)(2,1)S(1)}, u32[]{:S(2)}, u32[]{:S(2)}) async-start(bf16[2,256,2,512]{3,1,0,2:T(8,128)(2,1)} %copy.10), calls=%async_computation.2 | async-start | bytes 2097152 | tf_op jit(solution)/shard_map/all_to_all | solution.py:164
Sparse Core Ops, SparseCore 0:
  35.9 18.6 reduce-scatter.2
  82.0 19.0 reduce-scatter.2
  128.5 19.9 reduce-scatter.2
  175.9 20.8 reduce-scatter.2
  209.7 35.3 reduce-scatter.2
  258.0 35.3 reduce-scatter.2
  306.3 35.3 reduce-scatter.2
  362.8 44.4 reduce-scatter.4
  427.5 43.2 reduce-scatter.4
  491.1 43.2 reduce-scatter.4
  578.2 19.6 reduce-scatter.4
  641.7 19.7 reduce-scatter.4
  705.2 18.7 reduce-scatter.4
  767.9 17.8 reduce-scatter.4
Sparse Core Ops, SparseCore 1:
  801.6 109.1 all-gather.4
  912.8 102.0 all-gather.2
where the time goes:
time: 1030 us
  waiting for transfers between devices  615 us (60%)
  matrix products  169 us (16%)
  blocking collectives  138 us (13%)
  starting transfers between devices  36.5 us (4%)
  other arithmetic  33.5 us (3%)
  local copies, waits for them, and re-layouts  23.8 us (2%)
  between operations  15.3 us (1%)
    reduce_scatter x7, waiting for transfers between devices, backward_turn(): lax.psum_scatter(norm_part, 'mp', scatter_dimension=1, tiled=True)  208 us
    reduce_scatter x7, waiting for transfers between devices, forward_turn(): branch_sum = lax.psum_scatter(branch, 'mp', scatter_dimension=1, tiled=True)  186 us
    all_gather x1, waiting for transfers between devices, shards(): pregrad_piece = lax.all_gather(pregrad_all, 'dp', axis=0, tiled=True)  93.5 us
    all_gather x1, waiting for transfers between devices, shards(): activated_piece = lax.all_gather(activated_all, 'dp', axis=0, tiled=True)  81.4 us
    dot_general x4, matrix products, backward_active(): lax.dot_general(gathered, weight_second, CONTRACT_LAST, preferred_element...  50.5 us
    ppermute x14, waiting for transfers between devices, shifted(): return lax.ppermute(shard, axis, pairs)  44.9 us
    dot_general x4, matrix products, backward_active(): lax.dot_general(pre_grad, weight_first, CONTRACT_LAST, preferred_element_...  43.8 us
    dot_general x4, matrix products, forward_active(): jnp.dot(normed, weight_first, preferred_element_type=jnp.float32)  41.4 us
  transfers between devices with their start and end apart: 31, of which 30 were waited for; matrix products, arithmetic and copies ran while one was open for 1% of the time, Pallas kernels for 0%

commit v1 on v0

--- a/solution.py
+++ b/solution.py
@@ -163,8 +163,13 @@
     packed = jnp.stack((normed_all, outgrad_all)).reshape(2, all_rows, replicas, half_width)
     swapped = lax.all_to_all(packed, "dp", split_axis=2, concat_axis=1, tiled=True)
     columns = swapped.reshape(2, replicas * all_rows, half_width)
-    pregrad_piece = lax.all_gather(pregrad_all, "dp", axis=0, tiled=True)
-    activated_piece = lax.all_gather(activated_all, "dp", axis=0, tiled=True)
+    pregrad_piece, activated_piece = jnp.split(
+        lax.all_gather(
+            jnp.concatenate([pregrad_all, activated_all], axis=1), "dp", tiled=True, axis=0
+        ),
+        [pregrad_all.shape[1]],
+        axis=1,
+    )
     normed_cols = columns[0]
     outgrad_cols = columns[1]
     in_term = lax.dot_general(

time: 1030 us -> 1040 us (level)
    all_gather x2 -> x1, waiting for transfers between devices: 175 us -> 176 us  [shards(): lax.all_gather(jnp.concatenate([pregrad_all, activated_all], axis=1), 'dp...]
  transfers between devices with their start and end apart: 31 -> 30, of which waited for: 30 -> 29; matrix products, arithmetic and copies ran while one was open for 1% -> 0% of each run, Pallas kernels for 0% -> 0%
where the time goes in v1:
time: 1040 us; the launch traced here: 1030 us
  waiting for transfers between devices  615 us (59%)
  matrix products  168 us (16%)
  blocking collectives  133 us (13%)
  other arithmetic  41.3 us (4%)
  starting transfers between devices  36.6 us (4%)
  local copies, waits for them, and re-layouts  23.8 us (2%)
  between operations  15.2 us (1%)
    reduce_scatter x7, waiting for transfers between devices, backward_turn(): lax.psum_scatter(norm_part, 'mp', scatter_dimension=1, tiled=True)  208 us
    reduce_scatter x7, waiting for transfers between devices, forward_turn(): branch_sum = lax.psum_scatter(branch, 'mp', scatter_dimension=1, tiled=True)  186 us
    all_gather x1, waiting for transfers between devices, shards(): lax.all_gather(jnp.concatenate([pregrad_all, activated_all], axis=1), 'dp...  176 us
    dot_general x4, matrix products, backward_active(): lax.dot_general(gathered, weight_second, CONTRACT_LAST, preferred_element...  50.5 us
    ppermute x14, waiting for transfers between devices, shifted(): return lax.ppermute(shard, axis, pairs)  44.9 us
    dot_general x4, matrix products, backward_active(): lax.dot_general(pre_grad, weight_first, CONTRACT_LAST, preferred_element_...  43.8 us
    dot_general x4, matrix products, forward_active(): jnp.dot(normed, weight_first, preferred_element_type=jnp.float32)  41.4 us
    psum x7, blocking collectives, backward_turn(): row_dot = lax.psum(jnp.sum(scaled * unit_own, axis=1), 'mp')  40.3 us
  transfers between devices with their start and end apart: 30, of which 29 were waited for; matrix products, arithmetic and copies ran while one was open for 0% of the time, Pallas kernels for 0%

profile of v1, /device:TPU:0, one launch (start us, length us, event | category | flops | bytes accessed | tf_op | source)
XLA Modules:
  0.0 1034.8 jit_solution(8562382189569789318)
XLA Ops:
  13.2 334.3 %while.42 = (s32[]{:T(128)}, bf16[64,256]{1,0:T(8,128)(2,1)S(1)}, bf16[4,64,1024]{2,1,0:T(8,128)(2,1)S(1)}, f32[4,64]{1,0:T(4,128)S(1)}, f32[4,64,8192]{2,1,0:T(...) while((s32[]{:T(128)}, bf16[64,256]{1,0:T(8,128)(2,1)S(1)}, ...), condition=%wide.region_5.6_spmd, body=%wide.region_0.5_spmd.sunk | while | flops 2152726528 | bytes 110303480 | solution.py:91
  14.0 6.5 all_gather.24
  20.5 14.5 %conditional.5 = (f32[64,1024]{1,0:T(8,128)S(1)}, bf16[4,64,1024]{2,1,0:T(8,128)(2,1)S(1)}, f32[4,64]{1,0:T(4,128)S(1)}, f32[4,64,8192]{2,1,0:T(8,128)}) conditional(s32[]{:T(128)} %convert_element_type.141, (bf16[4,64,1024]{2,1,0:T(8,128)(2,1)S(1)}, f32[4,64]{1,0:T(4,128)S(1)}, f32[4,64,8192]{2,1,0:T(8,128)}) %tuple.97, ...), branch_computations={%region_1.1_spmd, %region_2.3_spmd} | conditional | flops 2152660992 | bytes 107747168 | solution.py:74
  20.7 10.4 %bitcast_dynamic-update-slice_fusion = (f32[4,64,8192]{2,1,0:T(8,128)}, f32[64,8192]{1,0:T(8,128)S(1)}) fusion(f32[4,64,8192]{2,1,0:T(8,128)} %get-tuple-element.578, s32[]{:T(128)S(6)} %select_n.85, bf16[1024,8192]{1,0:T(8,128)(2,1)} %get-tuple-element.573, bf16[64,1024]{1,0:T(8,128)(2,1)S(1)} %get-tuple-element.571, f32[1024]{0:T(1024)S(1)} %bitcast.76, ...), kind=kOutput, calls=%fused_computation.6 | convolution fusion | flops 1074003968 | bytes 21106948 | tf_op jit(solution)/shard_map/while/body/eval_jaxpr/cond/branch_1_fun/dot_general | solution.py:57
  35.8 18.8 %reduce-scatter.3.cloned.1.call-done = f32[64,256]{1,0:T(8,128)} async-done(((f32[64,1024]{1,0:T(8,128)}), f32[64,256]{1,0:T(8,128)}) %reduce-scatter.3.cloned.1.call-update) | async-done | bytes 65552 | tf_op jit(solution)/shard_map/while/body/eval_jaxpr/reduce_scatter | solution.py:80
  61.1 5.4 all_gather.24
  66.5 14.5 %conditional.5 = (f32[64,1024]{1,0:T(8,128)S(1)}, bf16[4,64,1024]{2,1,0:T(8,128)(2,1)S(1)}, f32[4,64]{1,0:T(4,128)S(1)}, f32[4,64,8192]{2,1,0:T(8,128)}) conditional(s32[]{:T(128)} %convert_element_type.141, (bf16[4,64,1024]{2,1,0:T(8,128)(2,1)S(1)}, f32[4,64]{1,0:T(4,128)S(1)}, f32[4,64,8192]{2,1,0:T(8,128)}) %tuple.97, ...), branch_computations={%region_1.1_spmd, %region_2.3_spmd} | conditional | flops 2152660992 | bytes 107747168 | solution.py:74
  66.7 10.4 %bitcast_dynamic-update-slice_fusion = (f32[4,64,8192]{2,1,0:T(8,128)}, f32[64,8192]{1,0:T(8,128)S(1)}) fusion(f32[4,64,8192]{2,1,0:T(8,128)} %get-tuple-element.578, s32[]{:T(128)S(6)} %select_n.85, bf16[1024,8192]{1,0:T(8,128)(2,1)} %get-tuple-element.573, bf16[64,1024]{1,0:T(8,128)(2,1)S(1)} %get-tuple-element.571, f32[1024]{0:T(1024)S(1)} %bitcast.76, ...), kind=kOutput, calls=%fused_computation.6 | convolution fusion | flops 1074003968 | bytes 21106948 | tf_op jit(solution)/shard_map/while/body/eval_jaxpr/cond/branch_1_fun/dot_general | solution.py:57
  81.8 19.2 %reduce-scatter.3.cloned.1.call-done = f32[64,256]{1,0:T(8,128)} async-done(((f32[64,1024]{1,0:T(8,128)}), f32[64,256]{1,0:T(8,128)}) %reduce-scatter.3.cloned.1.call-update) | async-done | bytes 65552 | tf_op jit(solution)/shard_map/while/body/eval_jaxpr/reduce_scatter | solution.py:80
  107.6 5.4 all_gather.24
  113.0 14.5 %conditional.5 = (f32[64,1024]{1,0:T(8,128)S(1)}, bf16[4,64,1024]{2,1,0:T(8,128)(2,1)S(1)}, f32[4,64]{1,0:T(4,128)S(1)}, f32[4,64,8192]{2,1,0:T(8,128)}) conditional(s32[]{:T(128)} %convert_element_type.141, (bf16[4,64,1024]{2,1,0:T(8,128)(2,1)S(1)}, f32[4,64]{1,0:T(4,128)S(1)}, f32[4,64,8192]{2,1,0:T(8,128)}) %tuple.97, ...), branch_computations={%region_1.1_spmd, %region_2.3_spmd} | conditional | flops 2152660992 | bytes 107747168 | solution.py:74
  113.2 10.4 %bitcast_dynamic-update-slice_fusion = (f32[4,64,8192]{2,1,0:T(8,128)}, f32[64,8192]{1,0:T(8,128)S(1)}) fusion(f32[4,64,8192]{2,1,0:T(8,128)} %get-tuple-element.578, s32[]{:T(128)S(6)} %select_n.85, bf16[1024,8192]{1,0:T(8,128)(2,1)} %get-tuple-element.573, bf16[64,1024]{1,0:T(8,128)(2,1)S(1)} %get-tuple-element.571, f32[1024]{0:T(1024)S(1)} %bitcast.76, ...), kind=kOutput, calls=%fused_computation.6 | convolution fusion | flops 1074003968 | bytes 21106948 | tf_op jit(solution)/shard_map/while/body/eval_jaxpr/cond/branch_1_fun/dot_general | solution.py:57
  128.3 20.1 %reduce-scatter.3.cloned.1.call-done = f32[64,256]{1,0:T(8,128)} async-done(((f32[64,1024]{1,0:T(8,128)}), f32[64,256]{1,0:T(8,128)}) %reduce-scatter.3.cloned.1.call-update) | async-done | bytes 65552 | tf_op jit(solution)/shard_map/while/body/eval_jaxpr/reduce_scatter | solution.py:80
  155.0 5.4 all_gather.24
  160.4 14.5 %conditional.5 = (f32[64,1024]{1,0:T(8,128)S(1)}, bf16[4,64,1024]{2,1,0:T(8,128)(2,1)S(1)}, f32[4,64]{1,0:T(4,128)S(1)}, f32[4,64,8192]{2,1,0:T(8,128)}) conditional(s32[]{:T(128)} %convert_element_type.141, (bf16[4,64,1024]{2,1,0:T(8,128)(2,1)S(1)}, f32[4,64]{1,0:T(4,128)S(1)}, f32[4,64,8192]{2,1,0:T(8,128)}) %tuple.97, ...), branch_computations={%region_1.1_spmd, %region_2.3_spmd} | conditional | flops 2152660992 | bytes 107747168 | solution.py:74
  160.6 10.3 %bitcast_dynamic-update-slice_fusion = (f32[4,64,8192]{2,1,0:T(8,128)}, f32[64,8192]{1,0:T(8,128)S(1)}) fusion(f32[4,64,8192]{2,1,0:T(8,128)} %get-tuple-element.578, s32[]{:T(128)S(6)} %select_n.85, bf16[1024,8192]{1,0:T(8,128)(2,1)} %get-tuple-element.573, bf16[64,1024]{1,0:T(8,128)(2,1)S(1)} %get-tuple-element.571, f32[1024]{0:T(1024)S(1)} %bitcast.76, ...), kind=kOutput, calls=%fused_computation.6 | convolution fusion | flops 1074003968 | bytes 21106948 | tf_op jit(solution)/shard_map/while/body/eval_jaxpr/cond/branch_1_fun/dot_general | solution.py:57
  175.7 21.1 %reduce-scatter.3.cloned.1.call-done = f32[64,256]{1,0:T(8,128)} async-done(((f32[64,1024]{1,0:T(8,128)}), f32[64,256]{1,0:T(8,128)}) %reduce-scatter.3.cloned.1.call-update) | async-done | bytes 65552 | tf_op jit(solution)/shard_map/while/body/eval_jaxpr/reduce_scatter | solution.py:80
  203.3 5.4 all_gather.24
  209.5 35.6 %reduce-scatter.3.cloned.1.call-done = f32[64,256]{1,0:T(8,128)} async-done(((f32[64,1024]{1,0:T(8,128)}), f32[64,256]{1,0:T(8,128)}) %reduce-scatter.3.cloned.1.call-update) | async-done | bytes 65552 | tf_op jit(solution)/shard_map/while/body/eval_jaxpr/reduce_scatter | solution.py:80
  251.7 5.4 all_gather.24
  257.8 35.6 %reduce-scatter.3.cloned.1.call-done = f32[64,256]{1,0:T(8,128)} async-done(((f32[64,1024]{1,0:T(8,128)}), f32[64,256]{1,0:T(8,128)}) %reduce-scatter.3.cloned.1.call-update) | async-done | bytes 65552 | tf_op jit(solution)/shard_map/while/body/eval_jaxpr/reduce_scatter | solution.py:80
  300.0 5.4 all_gather.24
  306.1 35.6 %reduce-scatter.3.cloned.1.call-done = f32[64,256]{1,0:T(8,128)} async-done(((f32[64,1024]{1,0:T(8,128)}), f32[64,256]{1,0:T(8,128)}) %reduce-scatter.3.cloned.1.call-update) | async-done | bytes 65552 | tf_op jit(solution)/shard_map/while/body/eval_jaxpr/reduce_scatter | solution.py:80
  347.5 6.1 fusion.48
  356.2 443.2 %while.43 = (s32[]{:T(128)}, f32[64,256]{1,0:T(8,128)S(1)}, bf16[4,64,8192]{2,1,0:T(8,128)(2,1)}, bf16[4,64,1024]{2,1,0:T(8,128)(2,1)S(1)}, f32[256]{0:T(256)S(1...) while((s32[]{:T(128)}, f32[64,256]{1,0:T(8,128)S(1)}, ...), condition=%wide.region_13.14_spmd.clone, body=%wide.region_6.13_spmd.clone.sunk | while | flops 2157756928 | bytes 42672648 | solution.py:151
  356.3 5.4 all_gather.25
  362.5 44.6 %reduce-scatter.5.cloned.1.call-done = f32[64,256]{1,0:T(8,128)} async-done(((f32[64,1024]{1,0:T(8,128)}), f32[64,256]{1,0:T(8,128)}) %reduce-scatter.5.cloned.1.call-update) | async-done | bytes 65552 | tf_op jit(solution)/shard_map/while/body/eval_jaxpr/reduce_scatter | solution.py:135
  408.1 5.8 psum.23
  416.1 4.8 collective-permute-done.1
  420.9 5.4 all_gather.25
  427.2 43.4 %reduce-scatter.5.cloned.1.call-done = f32[64,256]{1,0:T(8,128)} async-done(((f32[64,1024]{1,0:T(8,128)}), f32[64,256]{1,0:T(8,128)}) %reduce-scatter.5.cloned.1.call-update) | async-done | bytes 65552 | tf_op jit(solution)/shard_map/while/body/eval_jaxpr/reduce_scatter | solution.py:135
  471.6 5.8 psum.23
  484.5 5.4 all_gather.25
  490.7 43.4 %reduce-scatter.5.cloned.1.call-done = f32[64,256]{1,0:T(8,128)} async-done(((f32[64,1024]{1,0:T(8,128)}), f32[64,256]{1,0:T(8,128)}) %reduce-scatter.5.cloned.1.call-update) | async-done | bytes 65552 | tf_op jit(solution)/shard_map/while/body/eval_jaxpr/reduce_scatter | solution.py:135
  535.2 5.8 psum.23
  548.0 5.4 all_gather.25
  553.5 23.6 %conditional.6 = (f32[64,1024]{1,0:T(8,128)S(1)}, bf16[4,64,8192]{2,1,0:T(8,128)(2,1)}, bf16[4,64,1024]{2,1,0:T(8,128)(2,1)S(1)}) conditional(s32[]{:T(128)} %convert_element_type.142, (bf16[4,64,8192]{2,1,0:T(8,128)(2,1)}, bf16[4,64,1024]{2,1,0:T(8,128)(2,1)S(1)}) %tuple.101, (bf16[64,1024]{1,0:T(8,128)(2,1)S(1)}, bf16[8192,1024]{1,0:T(8,128)(2,1)}, ...), branch_computations={%region_7.7_spmd, %region_8.8_spmd} | conditional | flops 2157445120 | bytes 39452740 | solution.py:126
  553.5 12.6 %bitcast_dynamic-update-slice_fusion.2 = (bf16[4,64,8192]{2,1,0:T(8,128)(2,1)}, bf16[64,8192]{1,0:T(8,128)(2,1)S(1)}) fusion(bf16[4,64,8192]{2,1,0:T(8,128)(2,1)} %get-tuple-element.602, s32[]{:T(128)S(6)} %select_n.88, f32[4,64,8192]{2,1,0:T(8,128)} %get-tuple-element.599, bf16[64,1024]{1,0:T(8,128)(2,1)S(1)} %get-tuple-element.597, ...), kind=kOutput, calls=%fused_computation.41 | convolution fusion | flops 1083703296 | bytes 21102596 | tf_op jit(solution)/shard_map/while/body/eval_jaxpr/cond/branch_1_fun/dot_general | solution.py:111
  566.1 10.9 %fusion.52 = f32[64,1024]{1,0:T(8,128)S(1)} fusion(bf16[64,8192]{1,0:T(8,128)(2,1)S(1)} %get-tuple-element.748, bf16[1024,8192]{1,0:T(8,128)(2,1)} %get-tuple-element.601), kind=kOutput, calls=%fused_computation.77 | convolution fusion | flops 1073741824 | bytes 18087936 | tf_op jit(solution)/shard_map/while/body/eval_jaxpr/cond/branch_1_fun/dot_general | solution.py:115
  577.8 19.8 %reduce-scatter.5.cloned.1.call-done = f32[64,256]{1,0:T(8,128)} async-done(((f32[64,1024]{1,0:T(8,128)}), f32[64,256]{1,0:T(8,128)}) %reduce-scatter.5.cloned.1.call-update) | async-done | bytes 65552 | tf_op jit(solution)/shard_map/while/body/eval_jaxpr/reduce_scatter | solution.py:135
  598.7 5.8 psum.23
  611.6 5.4 all_gather.25
  617.0 23.6 %conditional.6 = (f32[64,1024]{1,0:T(8,128)S(1)}, bf16[4,64,8192]{2,1,0:T(8,128)(2,1)}, bf16[4,64,1024]{2,1,0:T(8,128)(2,1)S(1)}) conditional(s32[]{:T(128)} %convert_element_type.142, (bf16[4,64,8192]{2,1,0:T(8,128)(2,1)}, bf16[4,64,1024]{2,1,0:T(8,128)(2,1)S(1)}) %tuple.101, (bf16[64,1024]{1,0:T(8,128)(2,1)S(1)}, bf16[8192,1024]{1,0:T(8,128)(2,1)}, ...), branch_computations={%region_7.7_spmd, %region_8.8_spmd} | conditional | flops 2157445120 | bytes 39452740 | solution.py:126
  617.0 12.6 %bitcast_dynamic-update-slice_fusion.2 = (bf16[4,64,8192]{2,1,0:T(8,128)(2,1)}, bf16[64,8192]{1,0:T(8,128)(2,1)S(1)}) fusion(bf16[4,64,8192]{2,1,0:T(8,128)(2,1)} %get-tuple-element.602, s32[]{:T(128)S(6)} %select_n.88, f32[4,64,8192]{2,1,0:T(8,128)} %get-tuple-element.599, bf16[64,1024]{1,0:T(8,128)(2,1)S(1)} %get-tuple-element.597, ...), kind=kOutput, calls=%fused_computation.41 | convolution fusion | flops 1083703296 | bytes 21102596 | tf_op jit(solution)/shard_map/while/body/eval_jaxpr/cond/branch_1_fun/dot_general | solution.py:111
  629.6 10.9 %fusion.52 = f32[64,1024]{1,0:T(8,128)S(1)} fusion(bf16[64,8192]{1,0:T(8,128)(2,1)S(1)} %get-tuple-element.748, bf16[1024,8192]{1,0:T(8,128)(2,1)} %get-tuple-element.601), kind=kOutput, calls=%fused_computation.77 | convolution fusion | flops 1073741824 | bytes 18087936 | tf_op jit(solution)/shard_map/while/body/eval_jaxpr/cond/branch_1_fun/dot_general | solution.py:115
  641.4 19.8 %reduce-scatter.5.cloned.1.call-done = f32[64,256]{1,0:T(8,128)} async-done(((f32[64,1024]{1,0:T(8,128)}), f32[64,256]{1,0:T(8,128)}) %reduce-scatter.5.cloned.1.call-update) | async-done | bytes 65552 | tf_op jit(solution)/shard_map/while/body/eval_jaxpr/reduce_scatter | solution.py:135
  662.2 5.8 psum.23
  675.1 5.4 all_gather.25
  680.5 23.6 %conditional.6 = (f32[64,1024]{1,0:T(8,128)S(1)}, bf16[4,64,8192]{2,1,0:T(8,128)(2,1)}, bf16[4,64,1024]{2,1,0:T(8,128)(2,1)S(1)}) conditional(s32[]{:T(128)} %convert_element_type.142, (bf16[4,64,8192]{2,1,0:T(8,128)(2,1)}, bf16[4,64,1024]{2,1,0:T(8,128)(2,1)S(1)}) %tuple.101, (bf16[64,1024]{1,0:T(8,128)(2,1)S(1)}, bf16[8192,1024]{1,0:T(8,128)(2,1)}, ...), branch_computations={%region_7.7_spmd, %region_8.8_spmd} | conditional | flops 2157445120 | bytes 39452740 | solution.py:126
  680.5 12.6 %bitcast_dynamic-update-slice_fusion.2 = (bf16[4,64,8192]{2,1,0:T(8,128)(2,1)}, bf16[64,8192]{1,0:T(8,128)(2,1)S(1)}) fusion(bf16[4,64,8192]{2,1,0:T(8,128)(2,1)} %get-tuple-element.602, s32[]{:T(128)S(6)} %select_n.88, f32[4,64,8192]{2,1,0:T(8,128)} %get-tuple-element.599, bf16[64,1024]{1,0:T(8,128)(2,1)S(1)} %get-tuple-element.597, ...), kind=kOutput, calls=%fused_computation.41 | convolution fusion | flops 1083703296 | bytes 21102596 | tf_op jit(solution)/shard_map/while/body/eval_jaxpr/cond/branch_1_fun/dot_general | solution.py:111
  693.2 11.0 %fusion.52 = f32[64,1024]{1,0:T(8,128)S(1)} fusion(bf16[64,8192]{1,0:T(8,128)(2,1)S(1)} %get-tuple-element.748, bf16[1024,8192]{1,0:T(8,128)(2,1)} %get-tuple-element.601), kind=kOutput, calls=%fused_computation.77 | convolution fusion | flops 1073741824 | bytes 18087936 | tf_op jit(solution)/shard_map/while/body/eval_jaxpr/cond/branch_1_fun/dot_general | solution.py:115
  704.9 18.9 %reduce-scatter.5.cloned.1.call-done = f32[64,256]{1,0:T(8,128)} async-done(((f32[64,1024]{1,0:T(8,128)}), f32[64,256]{1,0:T(8,128)}) %reduce-scatter.5.cloned.1.call-update) | async-done | bytes 65552 | tf_op jit(solution)/shard_map/while/body/eval_jaxpr/reduce_scatter | solution.py:135
  724.9 5.8 psum.23
  737.7 5.4 all_gather.25
  743.1 23.6 %conditional.6 = (f32[64,1024]{1,0:T(8,128)S(1)}, bf16[4,64,8192]{2,1,0:T(8,128)(2,1)}, bf16[4,64,1024]{2,1,0:T(8,128)(2,1)S(1)}) conditional(s32[]{:T(128)} %convert_element_type.142, (bf16[4,64,8192]{2,1,0:T(8,128)(2,1)}, bf16[4,64,1024]{2,1,0:T(8,128)(2,1)S(1)}) %tuple.101, (bf16[64,1024]{1,0:T(8,128)(2,1)S(1)}, bf16[8192,1024]{1,0:T(8,128)(2,1)}, ...), branch_computations={%region_7.7_spmd, %region_8.8_spmd} | conditional | flops 2157445120 | bytes 39452740 | solution.py:126
  743.1 12.6 %bitcast_dynamic-update-slice_fusion.2 = (bf16[4,64,8192]{2,1,0:T(8,128)(2,1)}, bf16[64,8192]{1,0:T(8,128)(2,1)S(1)}) fusion(bf16[4,64,8192]{2,1,0:T(8,128)(2,1)} %get-tuple-element.602, s32[]{:T(128)S(6)} %select_n.88, f32[4,64,8192]{2,1,0:T(8,128)} %get-tuple-element.599, bf16[64,1024]{1,0:T(8,128)(2,1)S(1)} %get-tuple-element.597, ...), kind=kOutput, calls=%fused_computation.41 | convolution fusion | flops 1083703296 | bytes 21102596 | tf_op jit(solution)/shard_map/while/body/eval_jaxpr/cond/branch_1_fun/dot_general | solution.py:111
  755.8 11.0 %fusion.52 = f32[64,1024]{1,0:T(8,128)S(1)} fusion(bf16[64,8192]{1,0:T(8,128)(2,1)S(1)} %get-tuple-element.748, bf16[1024,8192]{1,0:T(8,128)(2,1)} %get-tuple-element.601), kind=kOutput, calls=%fused_computation.77 | convolution fusion | flops 1073741824 | bytes 18087936 | tf_op jit(solution)/shard_map/while/body/eval_jaxpr/cond/branch_1_fun/dot_general | solution.py:115
  767.5 18.0 %reduce-scatter.5.cloned.1.call-done = f32[64,256]{1,0:T(8,128)} async-done(((f32[64,1024]{1,0:T(8,128)}), f32[64,256]{1,0:T(8,128)}) %reduce-scatter.5.cloned.1.call-update) | async-done | bytes 65552 | tf_op jit(solution)/shard_map/while/body/eval_jaxpr/reduce_scatter | solution.py:135
  786.6 5.8 psum.23
  799.4 7.7 pad_maximum_fusion
  814.7 16.3 %psum.20 = f32[1,256]{1,0:T(1,128)} all-reduce(f32[1,256]{1,0:T(1,128)S(1)} %bitcast.80), channel_id=1, replica_groups=mesh['dp'=2,'pipe'=4,'mp'=4] {'dp'}, use_global_device_ids=true, to_apply=%region_14.15 | all-reduce | flops 256 | bytes 2048 | tf_op jit(solution)/shard_map/psum | solution.py:186
  831.1 176.2 %all-gather.2.cloned.1.call-done = bf16[512,16384]{1,0:T(8,128)(2,1)} async-done(((bf16[256,16384]{1,0:T(8,128)(2,1)}), bf16[512,16384]{1,0:T(8,128)(2,1)}) %all-gather.2.cloned.1.call-update) | async-done | bytes 16777232 | tf_op jit(solution)/shard_map/all_gather | solution.py:167
  1007.3 10.2 fusion.43
  1017.5 10.2 fusion.42
  (207 shorter events, 140.5 us)
Async XLA Ops:
  8.0 5.2 copy-start.3
  13.2 41.4 %reduce-scatter.3.cloned.1.call-start = ((), (), s32[]{:S(2)}) async-start(), calls=%async_computation.4 | async-start | bytes 327680 | tf_op jit(solution)/shard_map/while/body/eval_jaxpr/reduce_scatter | solution.py:80
  20.7 11.3 %copy-start = (bf16[8192,1024]{1,0:T(8,128)(2,1)S(1)}, bf16[8192,1024]{1,0:T(8,128)(2,1)}, u32[]{:S(2)}) copy-start(bf16[8192,1024]{1,0:T(8,128)(2,1)} %get-tuple-element.574) | copy-start | bytes 50331652 | tf_op jit(solution)/shard_map/while/body/eval_jaxpr/cond
  35.0 0.7 copy-start.1
  55.4 5.0 collective-permute-start
  60.4 40.7 %reduce-scatter.3.cloned.1.call-start = ((), (), s32[]{:S(2)}) async-start(), calls=%async_computation.4 | async-start | bytes 327680 | tf_op jit(solution)/shard_map/while/body/eval_jaxpr/reduce_scatter | solution.py:80
  66.7 11.3 %copy-start = (bf16[8192,1024]{1,0:T(8,128)(2,1)S(1)}, bf16[8192,1024]{1,0:T(8,128)(2,1)}, u32[]{:S(2)}) copy-start(bf16[8192,1024]{1,0:T(8,128)(2,1)} %get-tuple-element.574) | copy-start | bytes 50331652 | tf_op jit(solution)/shard_map/while/body/eval_jaxpr/cond
  81.1 0.7 copy-start.1
  101.9 5.0 collective-permute-start
  106.9 41.6 %reduce-scatter.3.cloned.1.call-start = ((), (), s32[]{:S(2)}) async-start(), calls=%async_computation.4 | async-start | bytes 327680 | tf_op jit(solution)/shard_map/while/body/eval_jaxpr/reduce_scatter | solution.py:80
  113.2 11.3 %copy-start = (bf16[8192,1024]{1,0:T(8,128)(2,1)S(1)}, bf16[8192,1024]{1,0:T(8,128)(2,1)}, u32[]{:S(2)}) copy-start(bf16[8192,1024]{1,0:T(8,128)(2,1)} %get-tuple-element.574) | copy-start | bytes 50331652 | tf_op jit(solution)/shard_map/while/body/eval_jaxpr/cond
  127.6 0.7 copy-start.1
  149.3 4.9 collective-permute-start
  154.3 42.5 %reduce-scatter.3.cloned.1.call-start = ((), (), s32[]{:S(2)}) async-start(), calls=%async_computation.4 | async-start | bytes 327680 | tf_op jit(solution)/shard_map/while/body/eval_jaxpr/reduce_scatter | solution.py:80
  160.6 11.3 %copy-start = (bf16[8192,1024]{1,0:T(8,128)(2,1)S(1)}, bf16[8192,1024]{1,0:T(8,128)(2,1)}, u32[]{:S(2)}) copy-start(bf16[8192,1024]{1,0:T(8,128)(2,1)} %get-tuple-element.574) | copy-start | bytes 50331652 | tf_op jit(solution)/shard_map/while/body/eval_jaxpr/cond
  175.0 0.7 copy-start.1
  197.6 5.0 collective-permute-start
  202.6 42.5 %reduce-scatter.3.cloned.1.call-start = ((), (), s32[]{:S(2)}) async-start(), calls=%async_computation.4 | async-start | bytes 327680 | tf_op jit(solution)/shard_map/while/body/eval_jaxpr/reduce_scatter | solution.py:80
  208.8 0.7 copy-start.1
  245.9 5.0 collective-permute-start
  250.9 42.5 %reduce-scatter.3.cloned.1.call-start = ((), (), s32[]{:S(2)}) async-start(), calls=%async_computation.4 | async-start | bytes 327680 | tf_op jit(solution)/shard_map/while/body/eval_jaxpr/reduce_scatter | solution.py:80
  257.1 0.7 copy-start.1
  294.2 5.0 collective-permute-start
  299.2 42.5 %reduce-scatter.3.cloned.1.call-start = ((), (), s32[]{:S(2)}) async-start(), calls=%async_computation.4 | async-start | bytes 327680 | tf_op jit(solution)/shard_map/while/body/eval_jaxpr/reduce_scatter | solution.py:80
  305.4 0.7 copy-start.1
  342.5 5.0 collective-permute-start
  347.5 8.7 copy-start.4
  356.2 50.8 %reduce-scatter.5.cloned.1.call-start = ((), (), s32[]{:S(2)}) async-start(), calls=%async_computation.5 | async-start | bytes 327680 | tf_op jit(solution)/shard_map/while/body/eval_jaxpr/reduce_scatter | solution.py:135
  361.7 0.7 copy-start.2
  414.8 6.2 collective-permute-start.1
  420.9 49.7 %reduce-scatter.5.cloned.1.call-start = ((), (), s32[]{:S(2)}) async-start(), calls=%async_computation.5 | async-start | bytes 327680 | tf_op jit(solution)/shard_map/while/body/eval_jaxpr/reduce_scatter | solution.py:135
  426.4 0.7 copy-start.2
  478.3 6.2 collective-permute-start.1
  484.5 49.7 %reduce-scatter.5.cloned.1.call-start = ((), (), s32[]{:S(2)}) async-start(), calls=%async_computation.5 | async-start | bytes 327680 | tf_op jit(solution)/shard_map/while/body/eval_jaxpr/reduce_scatter | solution.py:135
  490.0 0.7 copy-start.2
  541.9 6.2 collective-permute-start.1
  548.0 49.7 %reduce-scatter.5.cloned.1.call-start = ((), (), s32[]{:S(2)}) async-start(), calls=%async_computation.5 | async-start | bytes 327680 | tf_op jit(solution)/shard_map/while/body/eval_jaxpr/reduce_scatter | solution.py:135
  577.1 0.7 copy-start.2
  605.4 6.2 collective-permute-start.1
  611.6 49.6 %reduce-scatter.5.cloned.1.call-start = ((), (), s32[]{:S(2)}) async-start(), calls=%async_computation.5 | async-start | bytes 327680 | tf_op jit(solution)/shard_map/while/body/eval_jaxpr/reduce_scatter | solution.py:135
  640.6 0.7 copy-start.2
  668.9 6.2 collective-permute-start.1
  675.1 48.7 %reduce-scatter.5.cloned.1.call-start = ((), (), s32[]{:S(2)}) async-start(), calls=%async_computation.5 | async-start | bytes 327680 | tf_op jit(solution)/shard_map/while/body/eval_jaxpr/reduce_scatter | solution.py:135
  704.1 0.7 copy-start.2
  731.6 6.2 collective-permute-start.1
  737.7 47.8 %reduce-scatter.5.cloned.1.call-start = ((), (), s32[]{:S(2)}) async-start(), calls=%async_computation.5 | async-start | bytes 327680 | tf_op jit(solution)/shard_map/while/body/eval_jaxpr/reduce_scatter | solution.py:135
  766.8 0.7 copy-start.2
  793.3 6.2 collective-permute-start.1
  799.4 207.9 %all-gather.2.cloned.1.call-start = ((), (), s32[]{:S(2)}) async-start(), calls=%async_computation.3 | async-start | bytes 25165824 | tf_op jit(solution)/shard_map/all_gather | solution.py:167
  810.8 20.2 %all-to-all-start = ((bf16[2,256,2,512]{3,1,0,2:T(8,128)(2,1)}), bf16[2,256,2,512]{3,1,0,2:T(8,128)(2,1)S(1)}, u32[]{:S(2)}, u32[]{:S(2)}) async-start(bf16[2,256,2,512]{3,1,0,2:T(8,128)(2,1)} %copy.10), calls=%async_computation.2 | async-start | bytes 2097152 | tf_op jit(solution)/shard_map/all_to_all | solution.py:164
Sparse Core Ops, SparseCore 0:
  35.9 18.6 reduce-scatter.2
  81.9 19.0 reduce-scatter.2
  128.4 19.9 reduce-scatter.2
  175.8 20.8 reduce-scatter.2
  209.6 35.3 reduce-scatter.2
  257.9 35.3 reduce-scatter.2
  306.3 35.3 reduce-scatter.2
  362.6 44.4 reduce-scatter.4
  427.2 43.2 reduce-scatter.4
  490.8 43.2 reduce-scatter.4
  577.9 19.7 reduce-scatter.4
  641.5 19.6 reduce-scatter.4
  705.0 18.7 reduce-scatter.4
  767.6 17.8 reduce-scatter.4
Sparse Core Ops, SparseCore 1:
  807.3 200.0 all-gather.1
